TPU v7x, 32 devices: a whole 2x2x4 slice. The times are simulated.
32 devices in a mesh: groups: 2 (over y), tm: 4 (over z), head: 4 (over x, core).
Axes of the slice: x: 2, y: 2, z: 4, core: 2. Of those that a mesh axis runs over, the one named last changes fastest.
Arguments:
- queries: bfloat16 [8, 256, 3072], P(('groups', 'tm'), 'head'), parts along dimension 0, may hold values from -128 to 128
- keys: bfloat16 [8, 256, 3072], P(('groups', 'tm'), 'head'), parts along dimension 0, may hold values from -6 to 6
- values: bfloat16 [8, 256, 3072], P(('groups', 'tm'), 'head'), parts along dimension 0, may hold values from -6 to 6
- residual: bfloat16 [8, 256, 5120], P(('groups', 'tm'), None, 'head'), parts along dimension 0, may hold values from -3 to 3
- fresh_frame: bfloat16 [512, 5120], P('groups', 'head'), parts along dimension 0, may hold values from -6 to 6
- out_weight: bfloat16 [3072, 5120], P('tm', 'head'), may hold values from -0.875 to 0.875
- time_weight: bfloat16 [256, 5120], P(None, 'head'), may hold values from -0.375 to 0.375
- noise_steps: int32 [8], P(('groups', 'tm')), parts along dimension 0, may hold values from 0 to 49, as said below
- frame_mask: int32 [8, 4], P(('groups', 'tm')), parts along dimension 0, may hold values from 0 to 1, as said below
Outputs:
- rolled: bfloat16 [8, 256, 5120], P(('groups', 'tm'), None, 'head'), parts along dimension 0
There are 2 independent parts, one for each index of `groups`. A program takes and returns all parts, laid end to end along the dimension named above; an argument that names none is the same for every part. Nothing has to cross between parts.
Inputs may be any that keep to these rules, and one draw needn't show every extreme that they name: frame_mask[i, j] is 1 exactly for i - L_i < j <= i, with a whole number L_i from 1 to 4 for each frame i; the last frame has L_i = 4. `noise_steps`: never falling along the frames; the first frame has 0 and the last 49.
All inputs are finite; a program needn't handle non-finite values.
Results may differ from a plain program's by a relative error of at most 0.0065.
Values may be sent and summed in bfloat16 or wider, within the bound.
A program may use at most 64 MiB of HBM per device.

v0:
```python
import math
import jax
import jax.numpy as jnp
from jax import lax
from jax.sharding import PartitionSpec as P

HD = 128
FREQ = 256
STEPS = 50


def shifted(value, axis, steps):
    count = lax.axis_size(axis)
    leading, last = (max(0, -steps), min(count, count - steps))
    return lax.ppermute(value, axis, [(source, source + steps) for source in range(leading, last)])


def time_features(noise_steps):
    timestep = 1000.0 * (noise_steps.astype(jnp.float32) + 1.0) / STEPS
    half = FREQ // 2
    rates = jnp.exp(-math.log(10000.0) * jnp.arange(half).astype(jnp.float32) / half)
    angles = timestep[:, None] * rates[None, :]
    return jnp.concatenate([jnp.cos(angles), jnp.sin(angles)], axis=1)


def on_device(
    queries, keys, values, residual, fresh_frame, out_weight, time_weight, noise_steps, frame_mask
):
    query_local, key_local, value_local = (
        lax.all_to_all(queries, "head", split_axis=2, concat_axis=1, tiled=True),
        lax.all_to_all(keys, "head", split_axis=2, concat_axis=1, tiled=True),
        lax.all_to_all(values, "head", split_axis=2, concat_axis=1, tiled=True),
    )
    tokens = query_local.shape[1]
    heads_here = query_local.shape[2] // HD
    scale = 1.0 / math.sqrt(HD)
    query_heads = query_local[0].reshape(tokens, heads_here, HD)
    key_value = jnp.stack([key_local[0], value_local[0]], axis=0)
    frame = lax.axis_index("tm")
    frames_total = lax.axis_size("tm")
    window = min(8, frames_total)
    mask_row = frame_mask[0]
    columns = jnp.arange(mask_row.shape[0], dtype=jnp.int32)

    def allowed_at(offset):
        hits = jnp.sum(jnp.where(columns == frame - offset, mask_row, 0))
        return hits > 0

    def absorb(state, block, allowed):
        running_max, weight_sum, accumulated = state
        key_heads = block[0].reshape(tokens, heads_here, HD)
        value_heads = block[1].reshape(tokens, heads_here, HD)
        scores = (
            jnp.einsum("qhd,khd->hqk", query_heads, key_heads, preferred_element_type=jnp.float32)
            * scale
        )
        new_max = jnp.where(allowed, jnp.maximum(running_max, jnp.max(scores, axis=2)), running_max)
        lifted = jnp.where(allowed, jnp.exp(jnp.minimum(scores - new_max[:, :, None], 0.0)), 0.0)
        factor = jnp.exp(running_max - new_max)
        weight_sum = weight_sum * factor + jnp.sum(lifted, axis=2)
        rounded = lifted.astype(jnp.bfloat16)
        accumulated = accumulated * jnp.transpose(factor)[:, :, None] + jnp.einsum(
            "hqk,khd->qhd", rounded, value_heads, preferred_element_type=jnp.float32
        )
        return (new_max, weight_sum, accumulated)

    state = (
        jnp.full((heads_here, tokens), -1e30, jnp.float32),
        jnp.zeros((heads_here, tokens), jnp.float32),
        jnp.zeros((tokens, heads_here, HD), jnp.float32),
    )
    state = absorb(state, key_value, allowed_at(0))
    moving = key_value
    for offset in range(1, window):
        moving = shifted(moving, "tm", 1)
        state = absorb(state, moving, allowed_at(offset))
    running_max, weight_sum, accumulated = state
    attention = (
        (accumulated / jnp.transpose(weight_sum)[:, :, None])
        .reshape(tokens, heads_here * HD)
        .astype(jnp.bfloat16)
    )
    weight_cols = lax.all_gather(out_weight, "tm", axis=0, tiled=True)
    projected = jnp.dot(
        lax.all_gather(attention, "head", axis=1, tiled=True),
        weight_cols,
        preferred_element_type=jnp.float32,
    )
    gate = jnp.dot(
        time_features(noise_steps), time_weight.astype(jnp.float32), precision=lax.Precision.HIGHEST
    )
    updated = (residual[0].astype(jnp.float32) + gate * projected).astype(jnp.bfloat16)
    moved = shifted(updated, "tm", -1)
    rolled = jnp.where(frame == frames_total - 1, fresh_frame, moved)
    return rolled[None]


def solution(mesh):
    placed = (
        P(("groups", "tm"), "head", None),
        P(("groups", "tm"), "head", None),
        P(("groups", "tm"), "head", None),
        P(("groups", "tm"), None, "head"),
        P("groups", "head"),
        P("tm", "head"),
        P(None, "head"),
        P(("groups", "tm")),
        P(("groups", "tm"), None),
    )
    return jax.shard_map(
        on_device,
        mesh=mesh,
        in_specs=placed,
        out_specs=P(("groups", "tm"), None, "head"),
        check_vma=False,
    )
```

profile of v0, /device:TPU:0, one launch (start us, length us, event | category | flops | bytes accessed | tf_op | source)
XLA Modules:
  0.0 350.7 jit_solution(9926861367071621732)
XLA Ops:
  6.5 3.6 %copy.96 = bf16[1,64,3072]{1,0,2:T(2,128)(2,1)S(1)} copy(bf16[1,64,3072]{2,1,0:T(8,128)(2,1)} %param.10) | data formatting | bytes 786432 | tf_op args[1]
  10.2 0.5 broadcast.158
  10.7 16.9 %reduce.3 = bf16[3072,64]{1,0:T(8,128)(2,1)S(1)} reduce(bf16[3072,1,64]{2,1,0:T(2,128)(2,1)S(1)} %bitcast.180, bf16[]{:T(256)} %broadcast.158), dimensions={1}, to_apply=%bitcast.157.reduce_sub_computation | reduce | bytes 786434
  27.6 1.3 reshape.82
  28.9 4.2 %all-to-all-start.1 = ((bf16[4,2,24576]{2,1,0:T(2,128)(2,1)}), bf16[4,2,24576]{2,1,0:T(2,128)(2,1)S(1)}, u32[]{:S(2)}, u32[]{:S(2)}) async-start(bf16[4,2,24576]{2,1,0:T(2,128)(2,1)} %reshape.82), calls=%async_computation.1 | async-start | bytes 786432 | tf_op jit(solution)/shard_map/all_to_all | solution.py:31
  33.1 3.6 %copy.102 = bf16[1,64,3072]{1,0,2:T(2,128)(2,1)S(1)} copy(bf16[1,64,3072]{2,1,0:T(8,128)(2,1)} %param.11) | data formatting | bytes 786432 | tf_op args[2]
  36.7 16.9 %reduce.2 = bf16[3072,64]{1,0:T(8,128)(2,1)S(1)} reduce(bf16[3072,1,64]{2,1,0:T(2,128)(2,1)S(1)} %bitcast.182, bf16[]{:T(256)} %broadcast.158), dimensions={1}, to_apply=%bitcast.155.reduce_sub_computation | reduce | bytes 786434
  53.6 1.3 reshape.80
  54.9 3.6 %all-to-all-start.2 = ((bf16[4,2,24576]{2,1,0:T(2,128)(2,1)}), bf16[4,2,24576]{2,1,0:T(2,128)(2,1)S(1)}, u32[]{:S(2)}, u32[]{:S(2)}) async-start(bf16[4,2,24576]{2,1,0:T(2,128)(2,1)} %reshape.80), calls=%async_computation.2 | async-start | bytes 786432 | tf_op jit(solution)/shard_map/all_to_all | solution.py:32
  58.5 0.8 reshape.83
  59.3 1.5 copy.97
  60.8 0.3 all_to_all.41
  61.2 4.8 %all-to-all-done.2 = bf16[4,2,24576]{2,1,0:T(2,128)(2,1)S(1)} async-done(((bf16[4,2,24576]{2,1,0:T(2,128)(2,1)}), bf16[4,2,24576]{2,1,0:T(2,128)(2,1)S(1)}, u32[]{:S(2)}, u32[]{:S(2)}) %all-to-all-start.2) | async-done | bytes 393248 | tf_op jit(solution)/shard_map/all_to_all | solution.py:32
  65.9 0.8 reshape.81
  66.7 1.5 copy.103
  68.3 0.3 all_to_all.44
  68.6 0.9 pad_maximum_fusion
  69.5 5.1 %collective-permute-start = (bf16[2,256,768]{2,1,0:T(8,128)(2,1)}, bf16[2,256,768]{2,1,0:T(8,128)(2,1)}, u32[]{:S(2)}, u32[]{:S(2)}) collective-permute-start(bf16[2,256,768]{2,1,0:T(8,128)(2,1)} %pad_maximum_fusion), channel_id=1, source_target_pairs={{0,4},{4,8},{8,12},{1,5},{5,9},{9,13},{2,6},{6,10},{10,14},{3,7},{... | collective-permute-start | bytes 2359304 | tf_op jit(solution)/shard_map/ppermute | solution.py:15
  74.6 1.8 copy.93
  76.4 17.8 %reduce.4 = bf16[3072,64]{1,0:T(8,128)(2,1)} reduce(bf16[3072,1,64]{2,1,0:T(2,128)(2,1)S(1)} %bitcast.181, bf16[]{:T(256)} %broadcast.158), dimensions={1}, to_apply=%bitcast.159.reduce_sub_computation | reduce | bytes 786434
  94.2 2.4 reshape.84
  96.7 3.5 all-to-all-start
  100.2 3.7 %collective-permute-start.1 = (bf16[2,256,768]{2,1,0:T(8,128)(2,1)}, bf16[2,256,768]{2,1,0:T(8,128)(2,1)}, u32[]{:S(2)}, u32[]{:S(2)}) collective-permute-start(bf16[2,256,768]{2,1,0:T(8,128)(2,1)} %collective-permute-done), channel_id=1, source_target_pairs={{0,4},{4,8},{8,12},{1,5},{5,9},{9,13},{2,6},{6,10},{10,14},{3,7},{... | collective-permute-start | bytes 2359304 | tf_op jit(solution)/shard_map/ppermute | solution.py:15
  103.9 0.8 fusion.61
  107.3 1.2 reshape_squeeze_stack_squeeze.6
  108.5 0.6 copy.131
  109.2 0.8 reshape.85
  110.0 1.5 copy.94
  111.5 0.3 all_to_all.38
  111.9 0.5 reshape_squeeze.21
  112.3 1.2 reshape.78
  113.6 2.1 fusion.74
  115.7 1.2 fusion.73
  116.9 0.2 copy.109
  117.0 0.9 copy.112
  118.0 2.8 collective-permute-done.1
  120.7 5.3 %collective-permute-start.2 = (bf16[2,256,768]{2,1,0:T(8,128)(2,1)}, bf16[2,256,768]{2,1,0:T(8,128)(2,1)}, u32[]{:S(2)}, u32[]{:S(2)}) collective-permute-start(bf16[2,256,768]{2,1,0:T(8,128)(2,1)} %collective-permute-done.1), channel_id=1, source_target_pairs={{0,4},{4,8},{8,12},{1,5},{5,9},{9,13},{2,6},{6,10},{10,14},{3,7},{... | collective-permute-start | bytes 2359304 | tf_op jit(solution)/shard_map/ppermute | solution.py:15
  126.0 0.4 bitcast_reduce_fusion.2
  126.4 1.9 fusion.72
  128.3 1.2 copy.114
  129.5 0.9 copy.117
  130.5 1.6 bitcast_reduce_fusion.1
  132.0 9.9 %collective-permute-done.2 = bf16[2,256,768]{2,1,0:T(8,128)(2,1)} collective-permute-done((bf16[2,256,768]{2,1,0:T(8,128)(2,1)}, bf16[2,256,768]{2,1,0:T(8,128)(2,1)}, u32[]{:S(2)}, u32[]{:S(2)}) %collective-permute-start.2) | collective-permute-done | bytes 786464 | tf_op jit(solution)/shard_map/ppermute | solution.py:15
  141.9 1.9 fusion.71
  143.8 1.2 copy.119
  145.0 2.2 bitcast_reduce_fusion
  147.2 0.2 copy.122
  147.3 0.7 maximum_select_fusion
  148.1 2.2 fusion.20
  150.4 0.6 fusion.24
  151.1 0.7 copy-done.2
  151.9 0.4 fusion.18
  152.4 0.4 fusion.12
  152.8 0.5 copy-done.6
  153.4 0.4 fusion.14
  153.8 1.2 fusion.19
  155.1 0.7 all-gather.5.cloned.1.call-update
  156.5 0.4 convolution_reduce_fusion
  156.9 18.9 %all-gather.3.cloned.1.call-done = bf16[256,3072]{0,1:T(8,128)(2,1)} async-done(((bf16[256,768]{0,1:T(8,128)(2,1)}), bf16[256,3072]{0,1:T(8,128)(2,1)}) %all-gather.3.cloned.1.call-update) | async-done | bytes 1572880 | tf_op jit(solution)/shard_map/all_gather | solution.py:85
  175.8 142.6 %all-gather.5.cloned.1.call-done = bf16[3072,1280]{1,0:T(8,128)(2,1)} async-done(((bf16[768,1280]{1,0:T(8,128)(2,1)}), bf16[3072,1280]{1,0:T(8,128)(2,1)}) %all-gather.5.cloned.1.call-update) | async-done | bytes 7864336 | tf_op jit(solution)/shard_map/all_gather | solution.py:83
  318.5 6.0 %fusion.1 = bf16[256,1280]{1,0:T(8,128)(2,1)S(1)} fusion(bf16[256,3072]{0,1:T(8,128)(2,1)} %all-gather.3.cloned.1.call-done, bf16[3072,1280]{1,0:T(8,128)(2,1)} %all-gather.5.cloned.1.call-done, bf16[1,256,1280]{2,1,0:T(8,128)(2,1)S(1)} %copy-done.8, f32[1280]{0:T(1024)S(1)} %convolution_reduce_fusion), kind=kOutput, calls=%fused_computation.2 | convolution fusion | flops 2014576640 | bytes 10753024 | tf_op jit(solution)/shard_map/dot_general | solution.py:84
  324.4 1.3 collective-permute-start.3
  325.7 17.2 %collective-permute-done.3 = bf16[256,1280]{1,0:T(8,128)(2,1)S(1)} collective-permute-done((bf16[256,1280]{1,0:T(8,128)(2,1)S(1)}, bf16[256,1280]{1,0:T(8,128)(2,1)S(1)}, u32[]{:S(2)}, u32[]{:S(2)}) %collective-permute-start.3) | collective-permute-done | bytes 655392 | tf_op jit(solution)/shard_map/ppermute | solution.py:15
  343.0 0.9 select_bitcast_fusion
  (35 shorter events, 0.6 us)
Async XLA Ops:
  6.5 149.9 %copy-start = (bf16[256,1280]{1,0:T(8,128)(2,1)S(1)}, bf16[256,1280]{1,0:T(8,128)(2,1)}, u32[]{:S(2)}) copy-start(bf16[256,1280]{1,0:T(8,128)(2,1)} %param.15) | copy-start | bytes 1966084
  28.9 26.0 %all-to-all-start.1 = ((bf16[4,2,24576]{2,1,0:T(2,128)(2,1)}), bf16[4,2,24576]{2,1,0:T(2,128)(2,1)S(1)}, u32[]{:S(2)}, u32[]{:S(2)}) async-start(bf16[4,2,24576]{2,1,0:T(2,128)(2,1)} %reshape.82), calls=%async_computation.1 | async-start | bytes 786432 | tf_op jit(solution)/shard_map/all_to_all | solution.py:31
  54.9 11.1 %all-to-all-start.2 = ((bf16[4,2,24576]{2,1,0:T(2,128)(2,1)}), bf16[4,2,24576]{2,1,0:T(2,128)(2,1)S(1)}, u32[]{:S(2)}, u32[]{:S(2)}) async-start(bf16[4,2,24576]{2,1,0:T(2,128)(2,1)} %reshape.80), calls=%async_computation.2 | async-start | bytes 786432 | tf_op jit(solution)/shard_map/all_to_all | solution.py:32
  68.2 6.3 %copy-start.10 = (bf16[1,64,3072]{2,1,0:T(8,128)(2,1)S(1)}, bf16[1,64,3072]{2,1,0:T(8,128)(2,1)}, u32[]{:S(2)}) copy-start(bf16[1,64,3072]{2,1,0:T(8,128)(2,1)} %param.9) | copy-start | bytes 1179652
  69.5 30.7 %collective-permute-start = (bf16[2,256,768]{2,1,0:T(8,128)(2,1)}, bf16[2,256,768]{2,1,0:T(8,128)(2,1)}, u32[]{:S(2)}, u32[]{:S(2)}) collective-permute-start(bf16[2,256,768]{2,1,0:T(8,128)(2,1)} %pad_maximum_fusion), channel_id=1, source_target_pairs={{0,4},{4,8},{8,12},{1,5},{5,9},{9,13},{2,6},{6,10},{10,14},{3,7},{... | collective-permute-start | bytes 2359304 | tf_op jit(solution)/shard_map/ppermute | solution.py:15
  94.2 9.7 %copy-start.12 = (s32[1,4]{1,0:T(1,128)S(1)}, s32[1,4]{1,0:T(1,128)}, u32[]{:S(2)}) copy-start(s32[1,4]{1,0:T(1,128)} %param.17) | copy-start | bytes 52
  96.7 12.5 %all-to-all-start = ((bf16[4,2,24576]{2,1,0:T(2,128)(2,1)}), bf16[4,2,24576]{2,1,0:T(2,128)(2,1)S(1)}, u32[]{:S(2)}, u32[]{:S(2)}) async-start(bf16[4,2,24576]{2,1,0:T(2,128)(2,1)} %reshape.84), calls=%async_computation | async-start | bytes 786432 | tf_op jit(solution)/shard_map/all_to_all | solution.py:30
  100.1 75.7 %all-gather.3.cloned.1.call-start = ((), (), s32[]{:S(2)}) async-start(), calls=%async_computation.3 | async-start | bytes 1966080 | tf_op jit(solution)/shard_map/all_gather | solution.py:85
  100.2 20.5 %collective-permute-start.1 = (bf16[2,256,768]{2,1,0:T(8,128)(2,1)}, bf16[2,256,768]{2,1,0:T(8,128)(2,1)}, u32[]{:S(2)}, u32[]{:S(2)}) collective-permute-start(bf16[2,256,768]{2,1,0:T(8,128)(2,1)} %collective-permute-done), channel_id=1, source_target_pairs={{0,4},{4,8},{8,12},{1,5},{5,9},{9,13},{2,6},{6,10},{10,14},{3,7},{... | collective-permute-start | bytes 2359304 | tf_op jit(solution)/shard_map/ppermute | solution.py:15
  111.8 1.8 copy-start.4
  120.7 21.2 %collective-permute-start.2 = (bf16[2,256,768]{2,1,0:T(8,128)(2,1)}, bf16[2,256,768]{2,1,0:T(8,128)(2,1)}, u32[]{:S(2)}, u32[]{:S(2)}) collective-permute-start(bf16[2,256,768]{2,1,0:T(8,128)(2,1)} %collective-permute-done.1), channel_id=1, source_target_pairs={{0,4},{4,8},{8,12},{1,5},{5,9},{9,13},{2,6},{6,10},{10,14},{3,7},{... | collective-permute-start | bytes 2359304 | tf_op jit(solution)/shard_map/ppermute | solution.py:15
  148.1 2.2 copy-start.1
  148.1 2.3 copy-start.3
  150.4 0.7 copy-start.11
  150.4 1.4 copy-start.2
  150.4 1.5 copy-start.9
  151.1 1.3 copy-start.5
  152.4 1.0 copy-start.6
  155.0 163.5 %copy-start.8 = (bf16[1,256,1280]{2,1,0:T(8,128)(2,1)S(1)}, bf16[1,256,1280]{2,1,0:T(8,128)(2,1)}, u32[]{:S(2)}) copy-start(bf16[1,256,1280]{2,1,0:T(8,128)(2,1)} %param.12) | copy-start | bytes 1966084
  155.0 163.4 %all-gather.5.cloned.1.call-start = ((), (), s32[]{:S(2)}) async-start(), calls=%async_computation.4 | async-start | bytes 9830400 | tf_op jit(solution)/shard_map/all_gather | solution.py:83
  156.9 186.1 %copy-start.7 = (bf16[256,1280]{1,0:T(8,128)(2,1)S(1)}, bf16[256,1280]{1,0:T(8,128)(2,1)}, u32[]{:S(2)}) copy-start(bf16[256,1280]{1,0:T(8,128)(2,1)} %param.13) | copy-start | bytes 1966084
  324.4 18.5 %collective-permute-start.3 = (bf16[256,1280]{1,0:T(8,128)(2,1)S(1)}, bf16[256,1280]{1,0:T(8,128)(2,1)S(1)}, u32[]{:S(2)}, u32[]{:S(2)}) collective-permute-start(bf16[256,1280]{1,0:T(8,128)(2,1)S(1)} %fusion.1), channel_id=1, source_target_pairs={{4,0},{8,4},{12,8},{5,1},{9,5},{13,9},{6,2},{10,6},{14,10},{7,3},{... | collective-permute-start | bytes 1966088 | tf_op jit(solution)/shard_map/ppermute | solution.py:15
Sparse Core Ops, SparseCore 0:
  155.1 20.6 all-gather.2
  177.4 141.0 all-gather.4
where the time goes:
time: 352 us; the launch traced here: 351 us
  waiting for transfers between devices  197 us (56%)
  other arithmetic  57.8 us (16%)
  local copies, waits for them, and re-layouts  37.1 us (11%)
  starting transfers between devices  26.8 us (8%)
  between operations  17 us (5%)
  matrix products  15.1 us (4%)
    all_gather x1, waiting for transfers between devices, on_device(): weight_cols = lax.all_gather(out_weight, 'tm', axis=0, tiled=True)  143 us
    unnamed x3, other arithmetic  51.6 us
    ppermute x4, waiting for transfers between devices, shifted(): lax.ppermute(value, axis, [(source, source + steps) for source in range(l...  29.9 us
    all_gather x1, waiting for transfers between devices, on_device(): lax.all_gather(attention, 'head', axis=1, tiled=True)  18.9 us
    unnamed x36, local copies, waits for them, and re-layouts  18.5 us
    ppermute x4, starting transfers between devices, shifted(): lax.ppermute(value, axis, [(source, source + steps) for source in range(l...  15.3 us
  transfers between devices with their start and end apart: 9, of which 6 were waited for; matrix products, arithmetic and copies ran while one was open for 18% of the time, Pallas kernels for 0%

commit v1 on v0

--- a/solution.py
+++ b/solution.py
@@ -3,10 +3,31 @@
 import jax.numpy as jnp
 from jax import lax
 from jax.sharding import PartitionSpec as P
+from jax.lax import axis_index, axis_size, ppermute
 
 HD = 128
 FREQ = 256
 STEPS = 50
+
+
+def use_bars(own_rows, bus_axis):
+    num = axis_size(bus_axis)
+    heap = list(map(lambda s: (s, (s + 1) % num), range(num)))
+
+    def scan_cycles_over_axis(current_block):
+        if len(current_block) == num:
+            return current_block
+        view_out = scan_cycles_over_axis(
+            [ppermute(current_block[0], bus_axis, heap), *current_block]
+        )
+        return view_out
+
+    top = jnp.roll(
+        jnp.concatenate(scan_cycles_over_axis([own_rows]), 0),
+        (axis_index(bus_axis) + 1) * own_rows.shape[0],
+        axis=0,
+    )
+    return top
 
 
 def shifted(value, axis, steps):
@@ -80,7 +101,7 @@
         .reshape(tokens, heads_here * HD)
         .astype(jnp.bfloat16)
     )
-    weight_cols = lax.all_gather(out_weight, "tm", axis=0, tiled=True)
+    weight_cols = use_bars(out_weight, "tm")
     projected = jnp.dot(
         lax.all_gather(attention, "head", axis=1, tiled=True),
         weight_cols,

time: 352 us -> 291 us (0.83)
  waiting for transfers between devices: 197 us -> 114 us
  local copies, waits for them, and re-layouts: 37.1 us -> 58.1 us
  starting transfers between devices: 26.8 us -> 30.9 us
    all_gather x1 -> x0, waiting for transfers between devices: 143 us -> none  [on_device(): weight_cols = lax.all_gather(out_weight, 'tm', axis=0, tiled=True)]
    ppermute x4, waiting for transfers between devices: 29.9 us -> 71.3 us  [shifted(): lax.ppermute(value, axis, [(source, source + steps) for source in range(l...]
    ppermute x0 -> x3, waiting for transfers between devices: none -> 37.6 us  [scan_cycles_over_axis(): ppermute(current_block[0], bus_axis, heap)]
    unnamed x36 -> x47, local copies, waits for them, and re-layouts: 18.5 us -> 38.8 us
    all_gather x1, waiting for transfers between devices: 18.9 us -> 0.01 us  [on_device(): lax.all_gather(attention, 'head', axis=1, tiled=True)]
    ppermute x0 -> x3, starting transfers between devices: none -> 5.65 us  [scan_cycles_over_axis(): ppermute(current_block[0], bus_axis, heap)]
    all_to_all x1, waiting for transfers between devices: 4.77 us -> 0.01 us  [on_device(): lax.all_to_all(values, 'head', split_axis=2, concat_axis=1, tiled=True)]
    all_to_all x1, waiting for transfers between devices: 0.01 us -> 4.77 us  [on_device(): lax.all_to_all(keys, 'head', split_axis=2, concat_axis=1, tiled=True)]
  transfers between devices with their start and end apart: 9 -> 11, of which waited for: 6 -> 5; matrix products, arithmetic and copies ran while one was open for 18% -> 41% of each run, Pallas kernels for 0% -> 0%
where the time goes in v1:
time: 291 us; the launch traced here: 290 us
  waiting for transfers between devices  114 us (39%)
  local copies, waits for them, and re-layouts  58.1 us (20%)
  other arithmetic  55.5 us (19%)
  starting transfers between devices  30.9 us (11%)
  between operations  16.9 us (6%)
  matrix products  15.1 us (5%)
    ppermute x4, waiting for transfers between devices, shifted(): lax.ppermute(value, axis, [(source, source + steps) for source in range(l...  71.3 us
    unnamed x3, other arithmetic  51.6 us
    unnamed x47, local copies, waits for them, and re-layouts  38.8 us
    ppermute x3, waiting for transfers between devices, scan_cycles_over_axis(): ppermute(current_block[0], bus_axis, heap)  37.6 us
    ppermute x4, starting transfers between devices, shifted(): lax.ppermute(value, axis, [(source, source + steps) for source in range(l...  14.7 us
    slice x6, local copies, waits for them, and re-layouts, absorb(): value_heads = block[1].reshape(tokens, heads_here, HD)  8.13 us
    dot_general x1, matrix products, on_device(): jnp.dot(lax.all_gather(attention, 'head', axis=1, tiled=True), weight_col...  6.07 us
  transfers between devices with their start and end apart: 11, of which 5 were waited for; matrix products, arithmetic and copies ran while one was open for 41% of the time, Pallas kernels for 0%

profile of v1, /device:TPU:0, one launch (start us, length us, event | category | flops | bytes accessed | tf_op | source)
XLA Modules:
  0.0 290.2 jit_solution(8865766849988917208)
XLA Ops:
  6.5 3.1 %collective-permute-start.3 = (bf16[768,1280]{1,0:T(8,128)(2,1)}, bf16[768,1280]{1,0:T(8,128)(2,1)}, u32[]{:S(2)}, u32[]{:S(2)}) collective-permute-start(bf16[768,1280]{1,0:T(8,128)(2,1)} %param.14), channel_id=1, source_target_pairs={{0,4},{4,8},{8,12},{12,0},{1,5},{5,9},{9,13},{13,1},{2,6},{6,10},{... | collective-permute-start | bytes 5898248 | tf_op jit(solution)/shard_map/ppermute | solution.py:21
  9.6 3.6 %copy.102 = bf16[1,64,3072]{1,0,2:T(2,128)(2,1)S(1)} copy(bf16[1,64,3072]{2,1,0:T(8,128)(2,1)} %param.11) | data formatting | bytes 786432 | tf_op args[2]
  13.2 0.5 broadcast.158
  13.7 16.9 %reduce.2 = bf16[3072,64]{1,0:T(8,128)(2,1)S(1)} reduce(bf16[3072,1,64]{2,1,0:T(2,128)(2,1)S(1)} %bitcast.179, bf16[]{:T(256)} %broadcast.158), dimensions={1}, to_apply=%bitcast.155.reduce_sub_computation | reduce | bytes 786434
  30.6 1.3 reshape.80
  31.9 3.6 %all-to-all-start.2 = ((bf16[4,2,24576]{2,1,0:T(2,128)(2,1)}), bf16[4,2,24576]{2,1,0:T(2,128)(2,1)S(1)}, u32[]{:S(2)}, u32[]{:S(2)}) async-start(bf16[4,2,24576]{2,1,0:T(2,128)(2,1)} %reshape.80), calls=%async_computation.2 | async-start | bytes 786432 | tf_op jit(solution)/shard_map/all_to_all | solution.py:53
  35.5 3.6 %copy.96 = bf16[1,64,3072]{1,0,2:T(2,128)(2,1)S(1)} copy(bf16[1,64,3072]{2,1,0:T(8,128)(2,1)} %param.10) | data formatting | bytes 786432 | tf_op args[1]
  39.1 16.9 %reduce.3 = bf16[3072,64]{1,0:T(8,128)(2,1)S(1)} reduce(bf16[3072,1,64]{2,1,0:T(2,128)(2,1)S(1)} %bitcast.181, bf16[]{:T(256)} %broadcast.158), dimensions={1}, to_apply=%bitcast.157.reduce_sub_computation | reduce | bytes 786434
  56.0 1.3 reshape.82
  57.3 3.5 %all-to-all-start.1 = ((bf16[4,2,24576]{2,1,0:T(2,128)(2,1)}), bf16[4,2,24576]{2,1,0:T(2,128)(2,1)S(1)}, u32[]{:S(2)}, u32[]{:S(2)}) async-start(bf16[4,2,24576]{2,1,0:T(2,128)(2,1)} %reshape.82), calls=%async_computation.1 | async-start | bytes 786432 | tf_op jit(solution)/shard_map/all_to_all | solution.py:52
  60.8 0.8 reshape.81
  61.6 1.5 copy.103
  63.4 4.8 %all-to-all-done.1 = bf16[4,2,24576]{2,1,0:T(2,128)(2,1)S(1)} async-done(((bf16[4,2,24576]{2,1,0:T(2,128)(2,1)}), bf16[4,2,24576]{2,1,0:T(2,128)(2,1)S(1)}, u32[]{:S(2)}, u32[]{:S(2)}) %all-to-all-start.1) | async-done | bytes 393248 | tf_op jit(solution)/shard_map/all_to_all | solution.py:52
  68.1 0.8 reshape.83
  68.9 1.5 copy.97
  70.8 0.9 pad_maximum_fusion
  71.8 4.4 %collective-permute-start = (bf16[2,256,768]{2,1,0:T(8,128)(2,1)}, bf16[2,256,768]{2,1,0:T(8,128)(2,1)}, u32[]{:S(2)}, u32[]{:S(2)}) collective-permute-start(bf16[2,256,768]{2,1,0:T(8,128)(2,1)} %pad_maximum_fusion), channel_id=1, source_target_pairs={{0,4},{4,8},{8,12},{1,5},{5,9},{9,13},{2,6},{6,10},{10,14},{3,7},{... | collective-permute-start | bytes 2359304 | tf_op jit(solution)/shard_map/ppermute | solution.py:36
  76.2 1.8 copy.93
  78.0 17.8 %reduce.4 = bf16[3072,64]{1,0:T(8,128)(2,1)} reduce(bf16[3072,1,64]{2,1,0:T(2,128)(2,1)S(1)} %bitcast.180, bf16[]{:T(256)} %broadcast.158), dimensions={1}, to_apply=%bitcast.159.reduce_sub_computation | reduce | bytes 786434
  95.8 2.4 reshape.84
  98.2 3.5 %all-to-all-start = ((bf16[4,2,24576]{2,1,0:T(2,128)(2,1)}), bf16[4,2,24576]{2,1,0:T(2,128)(2,1)S(1)}, u32[]{:S(2)}, u32[]{:S(2)}) async-start(bf16[4,2,24576]{2,1,0:T(2,128)(2,1)} %reshape.84), calls=%async_computation | async-start | bytes 786432 | tf_op jit(solution)/shard_map/all_to_all | solution.py:51
  101.8 0.7 fusion.70
  105.6 3.8 %collective-permute-start.1 = (bf16[2,256,768]{2,1,0:T(8,128)(2,1)}, bf16[2,256,768]{2,1,0:T(8,128)(2,1)}, u32[]{:S(2)}, u32[]{:S(2)}) collective-permute-start(bf16[2,256,768]{2,1,0:T(8,128)(2,1)} %collective-permute-done), channel_id=1, source_target_pairs={{0,4},{4,8},{8,12},{1,5},{5,9},{9,13},{2,6},{6,10},{10,14},{3,7},{... | collective-permute-start | bytes 2359304 | tf_op jit(solution)/shard_map/ppermute | solution.py:36
  109.4 1.0 convolution_reduce_fusion
  110.4 0.5 reshape_squeeze_stack_squeeze.6
  110.9 0.8 reshape.85
  111.7 1.5 copy.94
  113.6 0.5 reshape_squeeze.21
  114.1 2.1 fusion.84
  116.2 0.6 copy.131
  116.9 1.2 reshape.78
  118.1 1.2 fusion.83
  119.4 0.9 copy.112
  120.4 6.4 %collective-permute-done.1 = bf16[2,256,768]{2,1,0:T(8,128)(2,1)} collective-permute-done((bf16[2,256,768]{2,1,0:T(8,128)(2,1)}, bf16[2,256,768]{2,1,0:T(8,128)(2,1)}, u32[]{:S(2)}, u32[]{:S(2)}) %collective-permute-start.1) | collective-permute-done | bytes 786464 | tf_op jit(solution)/shard_map/ppermute | solution.py:36
  126.7 5.3 %collective-permute-start.2 = (bf16[2,256,768]{2,1,0:T(8,128)(2,1)}, bf16[2,256,768]{2,1,0:T(8,128)(2,1)}, u32[]{:S(2)}, u32[]{:S(2)}) collective-permute-start(bf16[2,256,768]{2,1,0:T(8,128)(2,1)} %collective-permute-done.1), channel_id=1, source_target_pairs={{0,4},{4,8},{8,12},{1,5},{5,9},{9,13},{2,6},{6,10},{10,14},{3,7},{... | collective-permute-start | bytes 2359304 | tf_op jit(solution)/shard_map/ppermute | solution.py:36
  132.4 1.2 fusion.82
  133.8 0.9 copy.117
  134.7 1.5 bitcast_reduce_fusion.1
  136.2 49.0 %collective-permute-done.2 = bf16[2,256,768]{2,1,0:T(8,128)(2,1)} collective-permute-done((bf16[2,256,768]{2,1,0:T(8,128)(2,1)}, bf16[2,256,768]{2,1,0:T(8,128)(2,1)}, u32[]{:S(2)}, u32[]{:S(2)}) %collective-permute-start.2) | collective-permute-done | bytes 786464 | tf_op jit(solution)/shard_map/ppermute | solution.py:36
  185.1 2.1 fusion.81
  187.2 1.2 copy.119
  188.4 1.9 copy.122
  190.3 1.5 bitcast_reduce_fusion
  191.8 2.5 collective-permute-start.5
  194.3 0.6 fusion.33
  195.0 0.8 copy-done.4
  195.8 0.6 fusion.29
  197.4 0.4 fusion.21
  197.9 0.5 copy-done.6
  198.9 0.6 copy-done.8
  199.4 1.2 fusion.28
  200.6 37.6 %collective-permute-done.5 = bf16[768,1280]{1,0:T(8,128)(2,1)} collective-permute-done((bf16[768,1280]{1,0:T(8,128)(2,1)}, bf16[768,1280]{1,0:T(8,128)(2,1)}, u32[]{:S(2)}, u32[]{:S(2)}) %collective-permute-start.5) | collective-permute-done | bytes 1966112 | tf_op jit(solution)/shard_map/ppermute | solution.py:21
  238.3 3.0 %constant_dynamic-update-slice_fusion.7 = bf16[6144,1280]{1,0:T(8,128)(2,1)} fusion(bf16[768,1280]{1,0:T(8,128)(2,1)} %collective-permute-done.5), kind=kLoop, calls=%fused_computation.73 | loop fusion | bytes 3932160
  241.2 3.0 %constant_dynamic-update-slice_fusion.6 = bf16[6144,1280]{1,0:T(8,128)(2,1)} fusion(bf16[6144,1280]{1,0:T(8,128)(2,1)} %constant_dynamic-update-slice_fusion.7, bf16[768,1280]{1,0:T(8,128)(2,1)} %collective-permute-done.4), kind=kLoop, calls=%fused_computation.72 | loop fusion | bytes 3932160
  244.2 3.1 %constant_dynamic-update-slice_fusion.5 = bf16[6144,1280]{1,0:T(8,128)(2,1)} fusion(bf16[6144,1280]{1,0:T(8,128)(2,1)} %constant_dynamic-update-slice_fusion.6, bf16[768,1280]{1,0:T(8,128)(2,1)} %collective-permute-done.3), kind=kLoop, calls=%fused_computation.71 | loop fusion | bytes 3932160
  247.3 1.4 constant_dynamic-update-slice_fusion.4
  248.7 3.0 %constant_dynamic-update-slice_fusion.3 = bf16[6144,1280]{1,0:T(8,128)(2,1)} fusion(bf16[6144,1280]{1,0:T(8,128)(2,1)} %constant_dynamic-update-slice_fusion.4, bf16[768,1280]{1,0:T(8,128)(2,1)} %collective-permute-done.5), kind=kLoop, calls=%fused_computation.69 | loop fusion | bytes 3932160
  251.7 2.9 %constant_dynamic-update-slice_fusion.2 = bf16[6144,1280]{1,0:T(8,128)(2,1)} fusion(bf16[6144,1280]{1,0:T(8,128)(2,1)} %constant_dynamic-update-slice_fusion.3, bf16[768,1280]{1,0:T(8,128)(2,1)} %collective-permute-done.4), kind=kLoop, calls=%fused_computation.68 | loop fusion | bytes 3932160
  254.6 3.1 %constant_dynamic-update-slice_fusion.1 = bf16[6144,1280]{1,0:T(8,128)(2,1)} fusion(bf16[6144,1280]{1,0:T(8,128)(2,1)} %constant_dynamic-update-slice_fusion.2, bf16[768,1280]{1,0:T(8,128)(2,1)} %collective-permute-done.3), kind=kLoop, calls=%fused_computation.67 | loop fusion | bytes 3932160
  257.7 1.4 constant_dynamic-update-slice_fusion
  259.1 6.1 %fusion.8 = bf16[256,1280]{1,0:T(8,128)(2,1)S(1)} fusion(bf16[256,3072]{0,1:T(8,128)(2,1)} %all-gather.2.cloned.1.call-done, bf16[6144,1280]{1,0:T(8,128)(2,1)} %constant_dynamic-update-slice_fusion, s32[]{:T(128)S(6)} %select_n.178, bf16[1,256,1280]{2,1,0:T(8,128)(2,1)S(1)} %copy-done.14, f32[1280]{0:T(1024)S(1)} %copy-done.12), kind=kOutput, calls=%fused_computation.4 | convolution fusion | flops 2014576640 | bytes 10753028 | tf_op jit(solution)/shard_map/dot_general | solution.py:105
  265.2 1.3 collective-permute-start.6
  266.5 15.9 %collective-permute-done.6 = bf16[256,1280]{1,0:T(8,128)(2,1)S(1)} collective-permute-done((bf16[256,1280]{1,0:T(8,128)(2,1)S(1)}, bf16[256,1280]{1,0:T(8,128)(2,1)S(1)}, u32[]{:S(2)}, u32[]{:S(2)}) %collective-permute-start.6) | collective-permute-done | bytes 655392 | tf_op jit(solution)/shard_map/ppermute | solution.py:36
  282.4 0.9 select_bitcast_fusion
  (50 shorter events, 3.4 us)
Async XLA Ops:
  6.5 102.9 %copy-start = (bf16[256,1280]{1,0:T(8,128)(2,1)S(1)}, bf16[256,1280]{1,0:T(8,128)(2,1)}, u32[]{:S(2)}) copy-start(bf16[256,1280]{1,0:T(8,128)(2,1)} %param.15) | copy-start | bytes 1966084
  6.5 107.5 %collective-permute-start.3 = (bf16[768,1280]{1,0:T(8,128)(2,1)}, bf16[768,1280]{1,0:T(8,128)(2,1)}, u32[]{:S(2)}, u32[]{:S(2)}) collective-permute-start(bf16[768,1280]{1,0:T(8,128)(2,1)} %param.14), channel_id=1, source_target_pairs={{0,4},{4,8},{8,12},{12,0},{1,5},{5,9},{9,13},{13,1},{2,6},{6,10},{... | collective-permute-start | bytes 5898248 | tf_op jit(solution)/shard_map/ppermute | solution.py:21
  31.9 25.4 %all-to-all-start.2 = ((bf16[4,2,24576]{2,1,0:T(2,128)(2,1)}), bf16[4,2,24576]{2,1,0:T(2,128)(2,1)S(1)}, u32[]{:S(2)}, u32[]{:S(2)}) async-start(bf16[4,2,24576]{2,1,0:T(2,128)(2,1)} %reshape.80), calls=%async_computation.2 | async-start | bytes 786432 | tf_op jit(solution)/shard_map/all_to_all | solution.py:53
  57.3 10.8 %all-to-all-start.1 = ((bf16[4,2,24576]{2,1,0:T(2,128)(2,1)}), bf16[4,2,24576]{2,1,0:T(2,128)(2,1)S(1)}, u32[]{:S(2)}, u32[]{:S(2)}) async-start(bf16[4,2,24576]{2,1,0:T(2,128)(2,1)} %reshape.82), calls=%async_computation.1 | async-start | bytes 786432 | tf_op jit(solution)/shard_map/all_to_all | solution.py:52
  70.7 5.4 %copy-start.10 = (bf16[1,64,3072]{2,1,0:T(8,128)(2,1)S(1)}, bf16[1,64,3072]{2,1,0:T(8,128)(2,1)}, u32[]{:S(2)}) copy-start(bf16[1,64,3072]{2,1,0:T(8,128)(2,1)} %param.9) | copy-start | bytes 1179652
  71.8 33.8 %collective-permute-start = (bf16[2,256,768]{2,1,0:T(8,128)(2,1)}, bf16[2,256,768]{2,1,0:T(8,128)(2,1)}, u32[]{:S(2)}, u32[]{:S(2)}) collective-permute-start(bf16[2,256,768]{2,1,0:T(8,128)(2,1)} %pad_maximum_fusion), channel_id=1, source_target_pairs={{0,4},{4,8},{8,12},{1,5},{5,9},{9,13},{2,6},{6,10},{10,14},{3,7},{... | collective-permute-start | bytes 2359304 | tf_op jit(solution)/shard_map/ppermute | solution.py:36
  95.8 6.0 %copy-start.13 = (s32[1,4]{1,0:T(1,128)S(1)}, s32[1,4]{1,0:T(1,128)}, u32[]{:S(2)}) copy-start(s32[1,4]{1,0:T(1,128)} %param.17) | copy-start | bytes 52
  98.2 12.6 %all-to-all-start = ((bf16[4,2,24576]{2,1,0:T(2,128)(2,1)}), bf16[4,2,24576]{2,1,0:T(2,128)(2,1)S(1)}, u32[]{:S(2)}, u32[]{:S(2)}) async-start(bf16[4,2,24576]{2,1,0:T(2,128)(2,1)} %reshape.84), calls=%async_computation | async-start | bytes 786432 | tf_op jit(solution)/shard_map/all_to_all | solution.py:51
  101.7 157.4 %all-gather.2.cloned.1.call-start = ((), (), s32[]{:S(2)}) async-start(), calls=%async_computation.3 | async-start | bytes 1966080 | tf_op jit(solution)/shard_map/all_gather | solution.py:106
  105.6 21.1 %collective-permute-start.1 = (bf16[2,256,768]{2,1,0:T(8,128)(2,1)}, bf16[2,256,768]{2,1,0:T(8,128)(2,1)}, u32[]{:S(2)}, u32[]{:S(2)}) collective-permute-start(bf16[2,256,768]{2,1,0:T(8,128)(2,1)} %collective-permute-done), channel_id=1, source_target_pairs={{0,4},{4,8},{8,12},{1,5},{5,9},{9,13},{2,6},{6,10},{10,14},{3,7},{... | collective-permute-start | bytes 2359304 | tf_op jit(solution)/shard_map/ppermute | solution.py:36
  114.0 18.4 %copy-start.2 = (bf16[256,6,128]{2,1,0:T(8,128)(2,1)}, bf16[256,6,128]{2,1,0:T(8,128)(2,1)S(1)}, u32[]{:S(2)}) copy-start(bf16[256,6,128]{2,1,0:T(8,128)(2,1)S(1)} %reshape_squeeze.21) | copy-start | bytes 1179652
  114.0 77.8 %collective-permute-start.4 = (bf16[768,1280]{1,0:T(8,128)(2,1)}, bf16[768,1280]{1,0:T(8,128)(2,1)}, u32[]{:S(2)}, u32[]{:S(2)}) collective-permute-start(bf16[768,1280]{1,0:T(8,128)(2,1)} %collective-permute-done.3), channel_id=1, source_target_pairs={{0,4},{4,8},{8,12},{12,0},{1,5},{5,9},{9,13},{13,1},{2,6},{6,10},{... | collective-permute-start | bytes 5898248 | tf_op jit(solution)/shard_map/ppermute | solution.py:21
  126.7 58.4 %collective-permute-start.2 = (bf16[2,256,768]{2,1,0:T(8,128)(2,1)}, bf16[2,256,768]{2,1,0:T(8,128)(2,1)}, u32[]{:S(2)}, u32[]{:S(2)}) collective-permute-start(bf16[2,256,768]{2,1,0:T(8,128)(2,1)} %collective-permute-done.1), channel_id=1, source_target_pairs={{0,4},{4,8},{8,12},{1,5},{5,9},{9,13},{2,6},{6,10},{10,14},{3,7},{... | collective-permute-start | bytes 2359304 | tf_op jit(solution)/shard_map/ppermute | solution.py:36
  190.3 1.5 copy-start.11
  191.8 46.4 %collective-permute-start.5 = (bf16[768,1280]{1,0:T(8,128)(2,1)}, bf16[768,1280]{1,0:T(8,128)(2,1)}, u32[]{:S(2)}, u32[]{:S(2)}) collective-permute-start(bf16[768,1280]{1,0:T(8,128)(2,1)} %collective-permute-done.4), channel_id=1, source_target_pairs={{0,4},{4,8},{8,12},{12,0},{1,5},{5,9},{9,13},{13,1},{2,6},{6,10},{... | collective-permute-start | bytes 5898248 | tf_op jit(solution)/shard_map/ppermute | solution.py:21
  194.3 1.4 copy-start.4
  195.8 1.0 copy-start.9
  196.4 1.0 copy-start.5
  197.4 1.0 copy-start.6
  198.4 1.0 copy-start.8
  244.2 3.1 %copy-start.3 = (bf16[768,1280]{1,0:T(8,128)(2,1)S(1)}, bf16[768,1280]{1,0:T(8,128)(2,1)}, u32[]{:S(2)}) copy-start(bf16[768,1280]{1,0:T(8,128)(2,1)} %param.14) | copy-start | bytes 5898244
  257.7 1.4 copy-start.12
  257.7 1.4 copy-start.14
  259.1 23.3 %copy-start.7 = (bf16[256,1280]{1,0:T(8,128)(2,1)S(1)}, bf16[256,1280]{1,0:T(8,128)(2,1)}, u32[]{:S(2)}) copy-start(bf16[256,1280]{1,0:T(8,128)(2,1)} %param.13) | copy-start | bytes 1966084
  259.1 24.2 %copy-start.1 = (bf16[256,1280]{1,0:T(8,128)(2,1)S(1)}, bf16[256,1280]{1,0:T(8,128)(2,1)}, u32[]{:S(2)}) copy-start(bf16[256,1280]{1,0:T(8,128)(2,1)} %param.15) | copy-start | bytes 1966084
  265.2 17.2 %collective-permute-start.6 = (bf16[256,1280]{1,0:T(8,128)(2,1)S(1)}, bf16[256,1280]{1,0:T(8,128)(2,1)S(1)}, u32[]{:S(2)}, u32[]{:S(2)}) collective-permute-start(bf16[256,1280]{1,0:T(8,128)(2,1)S(1)} %fusion.8), channel_id=1, source_target_pairs={{4,0},{8,4},{12,8},{5,1},{9,5},{13,9},{6,2},{10,6},{14,10},{7,3},{... | collective-permute-start | bytes 1966088 | tf_op jit(solution)/shard_map/ppermute | solution.py:36
Sparse Core Ops, SparseCore 0:
  200.7 18.7 all-gather.1
